TPU v7x, 32 devices: a whole 2x2x4 slice. The times are simulated.
32 devices in a mesh: dp: 8 (over z, x), tm: 4 (over y, core).
Axes of the slice: x: 2, y: 2, z: 4, core: 2. Of those that a mesh axis runs over, the one named last changes fastest.
Arguments:
- frames: bfloat16 [8, 512, 1536], P('dp', 'tm'), may hold values from -3 to 3
- query: bfloat16 [8, 512, 1536], P('dp', 'tm'), may hold values from -6 to 6
- keys: bfloat16 [8, 512, 1536], P('dp', 'tm'), may hold values from -6 to 6
- values: bfloat16 [8, 512, 1536], P('dp', 'tm'), may hold values from -6 to 6
- norm_gain: float32 [1536], replicated, may hold values from 0.1 to 1.9
- conv_gain: float32 [1536], replicated, may hold values from 0.1 to 1.9
- w_glu: bfloat16 [1536, 3072], P('tm'), may hold values from -0.15625 to 0.15625
- taps: float32 [32, 1536], replicated, may hold values from -1 to 1
- w_out: bfloat16 [1536, 1536], P('tm'), may hold values from -0.15625 to 0.15625
- cotangent: bfloat16 [8, 512, 1536], P('dp', 'tm'), may hold values from -0.09375 to 0.09375
Outputs:
- glu_grad: float32 [1536, 3072], P('tm')
- taps_grad: float32 [32, 1536], P(None, 'tm')
- out_grad: float32 [1536, 1536], P('tm')
All inputs are finite; a program needn't handle non-finite values.
Results may differ from a plain program's by a relative error of at most 0.02.
Values may be sent and summed in bfloat16 or wider, within the bound.
No kernel may reach another device: no remote copies, remote signals or barrier semaphores. Data moves between devices by JAX's collectives and lax.ppermute only.
A program may use at most 128 MiB of HBM per device.

v0:
```python
import math
import jax
import jax.numpy as jnp
from jax import lax
from jax.sharding import PartitionSpec as P

HEADS = 16


def padded_2(value, sides, width):
    for axis, dim in sides:
        devices, length = (lax.axis_size(axis), value.shape[dim])
        up = [(i, (i + 1) % devices) for i in range(devices - 1)]
        down = [(j, i) for i, j in up]
        last = lax.slice_in_dim(value, length - width, length, axis=dim)
        leading = lax.slice_in_dim(value, 0, width, axis=dim)
        before = lax.ppermute(last, axis, up)
        after = lax.ppermute(leading, axis, down)
        value = jnp.concatenate([before, value, after], axis=dim)
    return value


def standard(v):
    mean = jnp.mean(v, axis=-1, keepdims=True)
    centred = v - mean
    var = jnp.mean(centred * centred, axis=-1, keepdims=True)
    inv = lax.rsqrt(var + 1e-05)
    return (centred * inv, inv)


def attend_heads(parts):
    q_all, k_all, v_all = parts
    length = q_all.shape[0]
    groups = q_all.shape[1]
    count = q_all.shape[2]
    head_dim = q_all.shape[3]
    q_flat = q_all.reshape(length, groups * count, head_dim)
    k_flat = k_all.reshape(length, groups * count, head_dim)
    v_flat = v_all.reshape(length, groups * count, head_dim)
    block = math.gcd(length, 512)
    scale = head_dim ** (-0.5)
    q_blocks = q_flat.reshape(length // block, block, groups * count, head_dim)

    def one_block(q_part):
        scores = (
            jnp.einsum("qhd,khd->hqk", q_part, k_flat, preferred_element_type=jnp.float32) * scale
        )
        top = jnp.max(scores, axis=2, keepdims=True)
        expo = jnp.exp(scores - top)
        total = jnp.sum(expo, axis=2)
        weights = expo.astype(jnp.bfloat16)
        summed = jnp.einsum("hqk,khd->qhd", weights, v_flat, preferred_element_type=jnp.float32)
        return (summed / total.T[:, :, None]).astype(jnp.bfloat16)

    return lax.map(one_block, q_blocks).reshape(length, groups, count, head_dim)


def add_rows(left, piece):
    return jnp.dot(left, piece, preferred_element_type=jnp.float32)


def project_back(cot_rows, piece):
    return lax.dot_general(
        cot_rows, piece, (((1,), (1,)), ((), ())), preferred_element_type=jnp.float32
    )


def rim_rows(field, half):
    return padded_2(field, (("tm", 0),), half)


def row_product(left, right):
    return lax.dot_general(
        left, right, (((0,), (0,)), ((), ())), preferred_element_type=jnp.float32
    )


def local(frames, query, keys, values, norm_gain, conv_gain, w_glu, taps, w_out, cotangent):
    rows = frames.shape[1]
    width = frames.shape[2]
    head_dim = width // HEADS
    groups = lax.axis_size("tm")
    per_group = HEADS // groups
    kernel = taps.shape[0]
    half = kernel // 2

    def split_heads(arr):
        return arr[0].reshape(rows, groups, per_group, head_dim)

    heads_out = attend_heads(
        (
            lax.all_to_all(split_heads(query), "tm", split_axis=1, concat_axis=0, tiled=True),
            lax.all_to_all(split_heads(keys), "tm", split_axis=1, concat_axis=0, tiled=True),
            lax.all_to_all(split_heads(values), "tm", split_axis=1, concat_axis=0, tiled=True),
        )
    )
    attention = lax.all_to_all(heads_out, "tm", split_axis=0, concat_axis=1, tiled=True).reshape(
        rows, width
    )
    mixed = frames[0].astype(jnp.float32) + attention.astype(jnp.float32)
    normed, unused = standard(mixed)
    u_rows = (normed * norm_gain).astype(jnp.bfloat16)
    p_full = add_rows(u_rows, lax.all_gather(w_glu, "tm", axis=0, tiled=True))
    first = p_full[:, :width]
    sig = jax.nn.sigmoid(p_full[:, width:])
    y_rows = (first * sig).astype(jnp.bfloat16)
    padded = rim_rows(y_rows, half)
    z_rows = jnp.zeros((rows, width), jnp.float32)
    for k in range(kernel):
        z_rows = z_rows + taps[k] * padded[k : k + rows].astype(jnp.float32)
    zhat, inv = standard(z_rows)
    n_rows = zhat * conv_gain
    sgate = jax.nn.sigmoid(n_rows)
    s_rows = (n_rows * sgate).astype(jnp.bfloat16)
    cot_rows = cotangent[0]
    d_s = project_back(cot_rows, lax.all_gather(w_out, "tm", axis=0, tiled=True))
    d_n = d_s * sgate * (1.0 + n_rows * (1.0 - sgate))
    e_rows = d_n * conv_gain
    d_z = (
        (
            e_rows
            - jnp.mean(e_rows, axis=-1, keepdims=True)
            - zhat * jnp.mean(e_rows * zhat, axis=-1, keepdims=True)
        )
        * inv
    ).astype(jnp.bfloat16)
    dz_pad = rim_rows(d_z, half)
    d_y = jnp.zeros((rows, width), jnp.float32)
    for k in range(kernel):
        d_y = d_y + taps[k] * dz_pad[2 * half - k : 2 * half - k + rows].astype(jnp.float32)
    d_p = jnp.concatenate([d_y * sig, d_y * first * sig * (1.0 - sig)], axis=1).astype(jnp.bfloat16)
    dz_float = d_z.astype(jnp.float32)
    taps_term = jnp.stack(
        [
            jnp.sum(dz_float * padded[k : k + rows].astype(jnp.float32), axis=0)
            for k in range(kernel)
        ]
    )
    glu_term = row_product(u_rows, d_p)
    glu_share, taps_share, out_share = (
        lax.psum_scatter(
            glu_term.astype(jnp.bfloat16), "tm", scatter_dimension=0, tiled=True
        ).astype(jnp.float32),
        lax.psum_scatter(
            taps_term.astype(jnp.bfloat16), "tm", scatter_dimension=1, tiled=True
        ).astype(jnp.float32),
        lax.psum_scatter(
            row_product(s_rows, cot_rows).astype(jnp.bfloat16),
            "tm",
            scatter_dimension=0,
            tiled=True,
        ).astype(jnp.float32),
    )
    glu_grad, taps_grad, out_grad = (
        lax.psum(glu_share.astype(jnp.bfloat16), "dp").astype(jnp.float32),
        lax.psum(taps_share.astype(jnp.bfloat16), "dp").astype(jnp.float32),
        lax.psum(out_share.astype(jnp.bfloat16), "dp").astype(jnp.float32),
    )
    return (glu_grad, taps_grad, out_grad)


def solution(mesh):
    return jax.shard_map(
        local,
        mesh=mesh,
        in_specs=(
            P("dp", "tm", None),
            P("dp", "tm", None),
            P("dp", "tm", None),
            P("dp", "tm", None),
            P(),
            P(),
            P("tm", None),
            P(),
            P("tm", None),
            P("dp", "tm", None),
        ),
        out_specs=(P("tm", None), P(None, "tm"), P("tm", None)),
        check_vma=False,
    )
```

profile of v0, /device:TPU:0, one launch (start us, length us, event | category | flops | bytes accessed | tf_op | source)
XLA Modules:
  0.0 441.2 jit_solution(16104276012726749351)
XLA Ops:
  8.7 1.9 copy.50
  10.6 4.3 all-to-all-start.1
  15.8 6.5 %all-to-all-done.1 = bf16[128,4,4,96]{0,3,2,1:T(8,128)(2,1)S(1)} async-done(((bf16[128,4,4,96]{0,3,2,1:T(8,128)(2,1)}), bf16[128,4,4,96]{0,3,2,1:T(8,128)(2,1)S(1)}, u32[]{:S(2)}, u32[]{:S(2)}) %all-to-all-start.1) | async-done | bytes 393248 | tf_op jit(solution)/shard_map/all_to_all | solution.py:93
  22.3 3.5 all-to-all-start
  26.7 11.1 %all-to-all-done = bf16[128,4,4,96]{0,3,2,1:T(8,128)(2,1)S(1)} async-done(((bf16[128,4,4,96]{0,3,2,1:T(8,128)(2,1)}), bf16[128,4,4,96]{0,3,2,1:T(8,128)(2,1)S(1)}, u32[]{:S(2)}, u32[]{:S(2)}) %all-to-all-start) | async-done | bytes 393248 | tf_op jit(solution)/shard_map/all_to_all | solution.py:92
  37.8 3.5 all-to-all-start.2
  42.2 11.1 %all-to-all-done.2 = bf16[128,4,4,96]{0,3,2,1:T(8,128)(2,1)S(1)} async-done(((bf16[128,4,4,96]{0,3,2,1:T(8,128)(2,1)}), bf16[128,4,4,96]{0,3,2,1:T(8,128)(2,1)S(1)}, u32[]{:S(2)}, u32[]{:S(2)}) %all-to-all-start.2) | async-done | bytes 393248 | tf_op jit(solution)/shard_map/all_to_all | solution.py:94
  56.1 1.1 copy.55
  57.2 3.6 all-to-all-start.3
  62.0 13.6 %all-to-all-done.3 = bf16[512,1,4,96]{3,2,1,0:T(4,128)(2,1)S(1)} async-done(((bf16[512,1,4,96]{3,2,1,0:T(4,128)(2,1)}), bf16[512,1,4,96]{3,2,1,0:T(4,128)(2,1)S(1)}, u32[]{:S(2)}, u32[]{:S(2)}) %all-to-all-start.3) | async-done | bytes 393248 | tf_op jit(solution)/shard_map/all_to_all | solution.py:97
  77.0 13.6 %all-gather.5.cloned.1.call-done = bf16[1536,3072]{1,0:T(8,128)(2,1)} async-done(((bf16[384,3072]{1,0:T(8,128)(2,1)}), bf16[1536,3072]{1,0:T(8,128)(2,1)}) %all-gather.5.cloned.1.call-update) | async-done | bytes 9437200 | tf_op jit(solution)/shard_map/all_gather | solution.py:103
  90.7 5.2 %fusion.179 = f32[128,3072]{1,0:T(8,128)S(1)} fusion(bf16[128,1536]{0,1:T(8,128)(2,1)S(1)} %multiply_convert_fusion.5, bf16[1536,3072]{1,0:T(8,128)(2,1)} %all-gather.5.cloned.1.call-done), kind=kOutput, calls=%fused_computation.372 | convolution fusion | flops 1207959552 | bytes 11403264 | tf_op jit(solution)/shard_map/dot_general | solution.py:59
  96.2 2.2 collective-permute-start
  98.4 1.3 collective-permute-start.1
  100.0 1.5 collective-permute-done.1
  101.7 4.1 fusion.175
  106.0 3.7 convolution_convert_fusion.1
  110.0 20.1 %all-gather.3.cloned.1.call-done = bf16[1536,1536]{1,0:T(8,128)(2,1)} async-done(((bf16[384,1536]{1,0:T(8,128)(2,1)}), bf16[1536,1536]{1,0:T(8,128)(2,1)}) %all-gather.3.cloned.1.call-update) | async-done | bytes 4718608 | tf_op jit(solution)/shard_map/all_gather | solution.py:116
  130.1 4.2 fusion.173
  134.4 4.4 fusion.98
  138.8 1.3 collective-permute-start.2
  140.1 3.0 collective-permute-start.3
  144.0 5.5 %multiply_convert_fusion.2 = (bf16[128,1536]{1,0:T(8,128)(2,1)S(1)}, f32[128,1536]{1,0:T(8,128)S(1)}) fusion(f32[128,3072]{1,0:T(8,128)S(1)} %fusion.179, bf16[128,1536]{1,0:T(8,128)(2,1)S(1)} %get-tuple-element.86, bf16[16,1536]{1,0:T(8,128)(2,1)S(1)} %collective-permute-done.3, f32[1536]{0:T(1024)} %copy-done.41, f32[1536]{0:T(1024)} %copy-done.42, ...), kind=kLoop, calls=%fused_computation.228 | loop fusion | flops 37945344 | bytes 2654208 | tf_op jit(solution)/shard_map/convert.68
  149.8 5.3 %convolution_convert_fusion = bf16[1536,3072]{1,0:T(8,128)(2,1)} fusion(bf16[128,1536]{0,1:T(8,128)(2,1)S(1)} %copy-done.2, bf16[128,1536]{1,0:T(8,128)(2,1)S(1)} %multiply_convert_fusion.1, bf16[128,1536]{1,0:T(8,128)(2,1)S(1)} %get-tuple-element.87), kind=kOutput, calls=%fused_computation | convolution fusion | flops 1214251008 | bytes 10616832 | tf_op jit(solution)/shard_map/dot_general | solution.py:73
  156.8 1.1 fusion.82
  160.6 20.7 %reduce-scatter.8.cloned.1.call-done = bf16[384,1536]{1,0:T(8,128)(2,1)} async-done(((bf16[1536,1536]{1,0:T(8,128)(2,1)}), bf16[384,1536]{1,0:T(8,128)(2,1)}) %reduce-scatter.8.cloned.1.call-update) | async-done | bytes 1179664 | tf_op jit(solution)/shard_map/reduce_scatter | solution.py:147
  181.3 80.4 %reduce-scatter.6.cloned.1.call-done = bf16[384,3072]{1,0:T(8,128)(2,1)} async-done(((bf16[1536,3072]{1,0:T(8,128)(2,1)}), bf16[384,3072]{1,0:T(8,128)(2,1)}) %reduce-scatter.6.cloned.1.call-update) | async-done | bytes 2359312 | tf_op jit(solution)/shard_map/reduce_scatter | solution.py:141
  261.7 23.7 %reduce-scatter.10.cloned.1.call-done = bf16[384,32]{1,0:T(8,128)(2,1)} async-done(((bf16[1536,32]{1,0:T(8,128)(2,1)}), bf16[384,32]{1,0:T(8,128)(2,1)}) %reduce-scatter.10.cloned.1.call-update) | async-done | bytes 24592
  286.4 39.0 %psum.22 = bf16[32,384]{1,0:T(8,128)(2,1)S(1)} all-reduce(bf16[32,384]{1,0:T(8,128)(2,1)S(1)} %copy.60), channel_id=1, replica_groups=mesh['dp'=8,'tm'=4] {'dp'}, use_global_device_ids=true, to_apply=%region_43.44 | all-reduce | flops 12288 | bytes 49152 | tf_op jit(solution)/shard_map/psum | solution.py:156
  326.1 102.1 %all-reduce.3.cloned.1.call-done = (bf16[384,3072]{1,0:T(8,128)(2,1)}, bf16[384,1536]{1,0:T(8,128)(2,1)}) async-done(((bf16[384,3072]{1,0:T(8,128)(2,1)}, bf16[384,1536]{1,0:T(8,128)(2,1)}), (bf16[384,3072]{1,0:T(8,128)(2,1)}, bf16[384,1536]{1,0:T(8,128)(2,1)})) %all-reduce.3.cloned.1.call-update) | async-done | bytes 3538960 | tf_op jit(solution)/shard_map/psum | solution.py:155
  428.2 4.5 %convert_element_type.362 = f32[384,3072]{1,0:T(8,128)} convert(bf16[384,3072]{1,0:T(8,128)(2,1)} %get-tuple-element.84) | non-fusion elementwise | flops 1179648 | bytes 7077888 | tf_op jit(solution)/shard_map/convert_element_type | solution.py:155
  432.7 1.7 convert_element_type.366
  (193 shorter events, 17.4 us)
Async XLA Ops:
  7.2 98.8 %copy-start = (bf16[1,128,1536]{2,1,0:T(8,128)(2,1)S(1)}, bf16[1,128,1536]{2,1,0:T(8,128)(2,1)}, u32[]{:S(2)}) copy-start(bf16[1,128,1536]{2,1,0:T(8,128)(2,1)} %param.19) | copy-start | bytes 1179652
  7.2 18.6 %copy-start.9 = (bf16[1,128,1536]{2,1,0:T(8,128)(2,1)S(1)}, bf16[1,128,1536]{2,1,0:T(8,128)(2,1)}, u32[]{:S(2)}) copy-start(bf16[1,128,1536]{2,1,0:T(8,128)(2,1)} %param.13) | copy-start | bytes 1179652
  7.2 83.4 %all-gather.5.cloned.1.call-start = ((), (), s32[]{:S(2)}) async-start(), calls=%async_computation.8 | async-start | bytes 11796480 | tf_op jit(solution)/shard_map/all_gather | solution.py:103
  7.9 122.2 %all-gather.3.cloned.1.call-start = ((), (), s32[]{:S(2)}) async-start(), calls=%async_computation.7 | async-start | bytes 5898240 | tf_op jit(solution)/shard_map/all_gather | solution.py:116
  10.6 11.7 %all-to-all-start.1 = ((bf16[128,4,4,96]{0,3,2,1:T(8,128)(2,1)}), bf16[128,4,4,96]{0,3,2,1:T(8,128)(2,1)S(1)}, u32[]{:S(2)}, u32[]{:S(2)}) async-start(bf16[128,4,4,96]{0,3,2,1:T(8,128)(2,1)} %bitcast.4), calls=%async_computation.1 | async-start | bytes 786432 | tf_op jit(solution)/shard_map/all_to_all | solution.py:93
  22.3 15.5 %all-to-all-start = ((bf16[128,4,4,96]{0,3,2,1:T(8,128)(2,1)}), bf16[128,4,4,96]{0,3,2,1:T(8,128)(2,1)S(1)}, u32[]{:S(2)}, u32[]{:S(2)}) async-start(bf16[128,4,4,96]{0,3,2,1:T(8,128)(2,1)} %bitcast.1), calls=%async_computation | async-start | bytes 786432 | tf_op jit(solution)/shard_map/all_to_all | solution.py:92
  37.8 15.5 %all-to-all-start.2 = ((bf16[128,4,4,96]{0,3,2,1:T(8,128)(2,1)}), bf16[128,4,4,96]{0,3,2,1:T(8,128)(2,1)S(1)}, u32[]{:S(2)}, u32[]{:S(2)}) async-start(bf16[128,4,4,96]{0,3,2,1:T(8,128)(2,1)} %bitcast.7), calls=%async_computation.2 | async-start | bytes 786432 | tf_op jit(solution)/shard_map/all_to_all | solution.py:94
  57.2 19.5 %copy-start.52 = (f32[1536]{0:T(1024)S(1)}, f32[1536]{0:T(1024)}, u32[]{:S(2)}) copy-start(f32[1536]{0:T(1024)} %param.14) | copy-start | bytes 18436
  57.2 18.4 %all-to-all-start.3 = ((bf16[512,1,4,96]{3,2,1,0:T(4,128)(2,1)}), bf16[512,1,4,96]{3,2,1,0:T(4,128)(2,1)S(1)}, u32[]{:S(2)}, u32[]{:S(2)}) async-start(bf16[512,1,4,96]{3,2,1,0:T(4,128)(2,1)} %copy.55), calls=%async_computation.3 | async-start | bytes 1048576 | tf_op jit(solution)/shard_map/all_to_all | solution.py:97
  60.8 120.5 %reduce-scatter.8.cloned.1.call-start = ((), (), s32[]{:S(2)}) async-start(), calls=%async_computation.10 | async-start | bytes 5898240 | tf_op jit(solution)/shard_map/reduce_scatter | solution.py:147
  77.0 18.9 %copy-start.1 = (bf16[128,1536]{0,1:T(8,128)(2,1)}, bf16[128,1536]{0,1:T(8,128)(2,1)S(1)}, u32[]{:S(2)}) copy-start(bf16[128,1536]{0,1:T(8,128)(2,1)S(1)} %multiply_convert_fusion.5) | copy-start | bytes 1179652
  96.2 3.8 collective-permute-start
  98.4 3.1 collective-permute-start.1
  99.9 34.4 %copy-start.31 = (f32[1536]{0:T(1024)}, f32[1536]{0:T(1024)S(1)}, u32[]{:S(2)}) copy-start(f32[1536]{0:T(1024)S(1)} %get-tuple-element.72) | copy-start | bytes 18436
  99.9 34.4 %copy-start.32 = (f32[1536]{0:T(1024)}, f32[1536]{0:T(1024)S(1)}, u32[]{:S(2)}) copy-start(f32[1536]{0:T(1024)S(1)} %get-tuple-element.73) | copy-start | bytes 18436
  99.9 34.4 %copy-start.33 = (f32[1536]{0:T(1024)}, f32[1536]{0:T(1024)S(1)}, u32[]{:S(2)}) copy-start(f32[1536]{0:T(1024)S(1)} %get-tuple-element.74) | copy-start | bytes 18436
  99.9 34.4 %copy-start.34 = (f32[1536]{0:T(1024)}, f32[1536]{0:T(1024)S(1)}, u32[]{:S(2)}) copy-start(f32[1536]{0:T(1024)S(1)} %get-tuple-element.75) | copy-start | bytes 18436
  99.9 34.4 %copy-start.35 = (f32[1536]{0:T(1024)}, f32[1536]{0:T(1024)S(1)}, u32[]{:S(2)}) copy-start(f32[1536]{0:T(1024)S(1)} %get-tuple-element.76) | copy-start | bytes 18436
  99.9 34.4 %copy-start.36 = (f32[1536]{0:T(1024)}, f32[1536]{0:T(1024)S(1)}, u32[]{:S(2)}) copy-start(f32[1536]{0:T(1024)S(1)} %get-tuple-element.77) | copy-start | bytes 18436
  100.0 34.4 %copy-start.37 = (f32[1536]{0:T(1024)}, f32[1536]{0:T(1024)S(1)}, u32[]{:S(2)}) copy-start(f32[1536]{0:T(1024)S(1)} %get-tuple-element.78) | copy-start | bytes 18436
  100.0 34.4 %copy-start.38 = (f32[1536]{0:T(1024)}, f32[1536]{0:T(1024)S(1)}, u32[]{:S(2)}) copy-start(f32[1536]{0:T(1024)S(1)} %get-tuple-element.79) | copy-start | bytes 18436
  100.0 34.4 %copy-start.39 = (f32[1536]{0:T(1024)}, f32[1536]{0:T(1024)S(1)}, u32[]{:S(2)}) copy-start(f32[1536]{0:T(1024)S(1)} %get-tuple-element.80) | copy-start | bytes 18436
  100.0 34.4 %copy-start.40 = (f32[1536]{0:T(1024)}, f32[1536]{0:T(1024)S(1)}, u32[]{:S(2)}) copy-start(f32[1536]{0:T(1024)S(1)} %get-tuple-element.81) | copy-start | bytes 18436
  100.0 34.4 %copy-start.41 = (f32[1536]{0:T(1024)}, f32[1536]{0:T(1024)S(1)}, u32[]{:S(2)}) copy-start(f32[1536]{0:T(1024)S(1)} %get-tuple-element.82) | copy-start | bytes 18436
  100.0 34.4 %copy-start.42 = (f32[1536]{0:T(1024)}, f32[1536]{0:T(1024)S(1)}, u32[]{:S(2)}) copy-start(f32[1536]{0:T(1024)S(1)} %get-tuple-element.83) | copy-start | bytes 18436
  105.8 24.4 %copy-start.53 = (f32[128]{0:T(128)}, f32[128]{0:T(128)S(1)}, u32[]{:S(2)}) copy-start(f32[128]{0:T(128)S(1)} %broadcast_multiply_fusion.2) | copy-start | bytes 1540
  106.0 24.1 %copy-start.54 = (f32[128]{0:T(128)}, f32[128]{0:T(128)S(1)}, u32[]{:S(2)}) copy-start(f32[128]{0:T(128)S(1)} %add_rsqrt_fusion) | copy-start | bytes 1540
  109.8 151.9 %reduce-scatter.6.cloned.1.call-start = ((), (), s32[]{:S(2)}) async-start(), calls=%async_computation.9 | async-start | bytes 11796480 | tf_op jit(solution)/shard_map/reduce_scatter | solution.py:141
  138.8 4.3 collective-permute-start.2
  140.1 3.9 collective-permute-start.3
  155.2 130.2 %reduce-scatter.10.cloned.1.call-start = ((), (), s32[]{:S(2)}) async-start(), calls=%async_computation.11 | async-start | bytes 491520
  160.5 267.6 %all-reduce.3.cloned.1.call-start = ((), (), s32[]{:S(2)}) async-start(), calls=%async_computation.12 | async-start | bytes 7077888 | tf_op jit(solution)/shard_map/psum | solution.py:155
  (37 other events, 292.9 us)
Sparse Core Ops, SparseCore 0:
  9.6 80.9 all-gather.4
  92.1 37.9 all-gather.2
  133.3 47.9 reduce-scatter.7
  183.7 77.9 reduce-scatter.5
  264.6 20.7 reduce-scatter.9
  288.9 139.1 all-reduce.2
where the time goes:
time: 442 us; the launch traced here: 441 us
  waiting for transfers between devices  307 us (69%)
  blocking collectives  39 us (9%)
  other arithmetic  25.7 us (6%)
  starting transfers between devices  23 us (5%)
  matrix products  20.1 us (5%)
  between operations  15.3 us (3%)
  local copies, waits for them, and re-layouts  11.5 us (3%)
    psum x1, waiting for transfers between devices, local(): lax.psum(glu_share.astype(jnp.bfloat16), 'dp').astype(jnp.float32)  102 us
    reduce_scatter x1, waiting for transfers between devices, local(): lax.psum_scatter(glu_term.astype(jnp.bfloat16), 'tm', scatter_dimension=0...  80.4 us
    psum x1, blocking collectives, local(): lax.psum(taps_share.astype(jnp.bfloat16), 'dp').astype(jnp.float32)  39 us
    unnamed x7, waiting for transfers between devices  25.2 us
    reduce_scatter x1, waiting for transfers between devices, local(): lax.psum_scatter(row_product(s_rows, cot_rows).astype(jnp.bfloat16), 'tm'...  20.7 us
    all_gather x1, waiting for transfers between devices, local(): lax.all_gather(w_out, 'tm', axis=0, tiled=True)  20.1 us
    all_to_all x1, waiting for transfers between devices, local(): lax.all_to_all(heads_out, 'tm', split_axis=0, concat_axis=1, tiled=True)  13.6 us
    all_gather x1, waiting for transfers between devices, local(): p_full = add_rows(u_rows, lax.all_gather(w_glu, 'tm', axis=0, tiled=True))  13.6 us
  transfers between devices with their start and end apart: 14, of which 12 were waited for; matrix products, arithmetic and copies ran while one was open for 11% of the time, Pallas kernels for 0%

commit v1 on v0

--- a/solution.py
+++ b/solution.py
@@ -152,7 +152,7 @@
         ).astype(jnp.float32),
     )
     glu_grad, taps_grad, out_grad = (
-        lax.psum(glu_share.astype(jnp.bfloat16), "dp").astype(jnp.float32),
+        jnp.sum(lax.all_gather(glu_share.astype(jnp.bfloat16), "dp"), axis=0).astype(jnp.float32),
         lax.psum(taps_share.astype(jnp.bfloat16), "dp").astype(jnp.float32),
         lax.psum(out_share.astype(jnp.bfloat16), "dp").astype(jnp.float32),
     )

time: 442 us -> 754 us (1.71)
  waiting for transfers between devices: 307 us -> 610 us
  other arithmetic: 25.7 us -> 33.6 us
    all_gather x0 -> x1, waiting for transfers between devices: none -> 360 us  [local(): lax.all_gather(glu_share.astype(jnp.bfloat16), 'dp')]
    psum x1, waiting for transfers between devices: 102 us -> 44.7 us  [local(): lax.psum(out_share.astype(jnp.bfloat16), 'dp').astype(jnp.float32)]
    reduce_sum x0 -> x1, other arithmetic: none -> 10.9 us  [local(): jnp.sum(lax.all_gather(glu_share.astype(jnp.bfloat16), 'dp'), axis=0)]
    unnamed x7 -> x8, waiting for transfers between devices: 25.2 us -> 25.2 us
  transfers between devices with their start and end apart: 14 -> 15, of which waited for: 12 -> 13; matrix products, arithmetic and copies ran while one was open for 11% -> 7% of each run, Pallas kernels for 0% -> 0%
where the time goes in v1:
time: 754 us; the launch traced here: 753 us
  waiting for transfers between devices  610 us (81%)
  blocking collectives  37.5 us (5%)
  other arithmetic  33.6 us (4%)
  starting transfers between devices  23 us (3%)
  matrix products  20.1 us (3%)
  between operations  15.7 us (2%)
  local copies, waits for them, and re-layouts  12.5 us (2%)
    all_gather x1, waiting for transfers between devices, local(): lax.all_gather(glu_share.astype(jnp.bfloat16), 'dp')  360 us
    reduce_scatter x1, waiting for transfers between devices, local(): lax.psum_scatter(glu_term.astype(jnp.bfloat16), 'tm', scatter_dimension=0...  80.3 us
    psum x1, waiting for transfers between devices, local(): lax.psum(out_share.astype(jnp.bfloat16), 'dp').astype(jnp.float32)  44.7 us
    psum x1, blocking collectives, local(): lax.psum(taps_share.astype(jnp.bfloat16), 'dp').astype(jnp.float32)  37.5 us
    unnamed x8, waiting for transfers between devices  25.2 us
    reduce_scatter x1, waiting for transfers between devices, local(): lax.psum_scatter(row_product(s_rows, cot_rows).astype(jnp.bfloat16), 'tm'...  22.8 us
    all_gather x1, waiting for transfers between devices, local(): lax.all_gather(w_out, 'tm', axis=0, tiled=True)  18.7 us
  transfers between devices with their start and end apart: 15, of which 13 were waited for; matrix products, arithmetic and copies ran while one was open for 7% of the time, Pallas kernels for 0%

profile of v1, /device:TPU:0, one launch (start us, length us, event | category | flops | bytes accessed | tf_op | source)
XLA Modules:
  0.0 752.8 jit_solution(11757101284727429977)
XLA Ops:
  8.7 1.9 copy.52
  10.6 4.3 all-to-all-start.2
  15.8 6.5 all-to-all-done.2
  22.3 3.5 all-to-all-start
  26.7 11.1 %all-to-all-done = bf16[128,4,4,96]{0,3,2,1:T(8,128)(2,1)S(1)} async-done(((bf16[128,4,4,96]{0,3,2,1:T(8,128)(2,1)}), bf16[128,4,4,96]{0,3,2,1:T(8,128)(2,1)S(1)}, u32[]{:S(2)}, u32[]{:S(2)}) %all-to-all-start) | async-done | bytes 393248 | tf_op jit(solution)/shard_map/all_to_all | solution.py:92
  37.8 3.5 all-to-all-start.1
  42.2 11.1 %all-to-all-done.1 = bf16[128,4,4,96]{0,3,2,1:T(8,128)(2,1)S(1)} async-done(((bf16[128,4,4,96]{0,3,2,1:T(8,128)(2,1)}), bf16[128,4,4,96]{0,3,2,1:T(8,128)(2,1)S(1)}, u32[]{:S(2)}, u32[]{:S(2)}) %all-to-all-start.1) | async-done | bytes 393248 | tf_op jit(solution)/shard_map/all_to_all | solution.py:93
  57.2 3.6 all-to-all-start.3
  62.0 13.6 %all-to-all-done.3 = bf16[512,1,4,96]{3,2,1,0:T(4,128)(2,1)S(1)} async-done(((bf16[512,1,4,96]{3,2,1,0:T(4,128)(2,1)}), bf16[512,1,4,96]{3,2,1,0:T(4,128)(2,1)S(1)}, u32[]{:S(2)}, u32[]{:S(2)}) %all-to-all-start.3) | async-done | bytes 393248 | tf_op jit(solution)/shard_map/all_to_all | solution.py:97
  77.0 13.6 %all-gather.7.cloned.1.call-done = bf16[1536,3072]{1,0:T(8,128)(2,1)} async-done(((bf16[384,3072]{1,0:T(8,128)(2,1)}), bf16[1536,3072]{1,0:T(8,128)(2,1)}) %all-gather.7.cloned.1.call-update) | async-done | bytes 9437200 | tf_op jit(solution)/shard_map/all_gather | solution.py:103
  90.7 5.2 fusion.179
  96.2 1.3 collective-permute-start.1
  97.5 3.0 collective-permute-start
  101.7 4.1 fusion.175
  106.9 3.7 convolution_convert_fusion.1
  110.9 18.7 %all-gather.5.cloned.1.call-done = bf16[1536,1536]{1,0:T(8,128)(2,1)} async-done(((bf16[384,1536]{1,0:T(8,128)(2,1)}), bf16[1536,1536]{1,0:T(8,128)(2,1)}) %all-gather.5.cloned.1.call-update) | async-done | bytes 4718608 | tf_op jit(solution)/shard_map/all_gather | solution.py:116
  129.9 4.2 fusion.173
  134.1 3.3 fusion.98
  137.5 2.1 collective-permute-start.3
  139.6 1.3 collective-permute-start.2
  140.9 2.1 collective-permute-done.2
  143.3 4.0 multiply_convert_fusion.2
  147.7 5.3 convolution_convert_fusion
  158.4 22.8 %reduce-scatter.8.cloned.1.call-done = bf16[384,1536]{1,0:T(8,128)(2,1)} async-done(((bf16[1536,1536]{1,0:T(8,128)(2,1)}), bf16[384,1536]{1,0:T(8,128)(2,1)}) %reduce-scatter.8.cloned.1.call-update) | async-done | bytes 1179664 | tf_op jit(solution)/shard_map/reduce_scatter | solution.py:147
  181.3 80.3 %reduce-scatter.6.cloned.1.call-done = bf16[384,3072]{1,0:T(8,128)(2,1)} async-done(((bf16[1536,3072]{1,0:T(8,128)(2,1)}), bf16[384,3072]{1,0:T(8,128)(2,1)}) %reduce-scatter.6.cloned.1.call-update) | async-done | bytes 2359312 | tf_op jit(solution)/shard_map/reduce_scatter | solution.py:141
  261.7 23.8 %reduce-scatter.10.cloned.1.call-done = bf16[384,32]{1,0:T(8,128)(2,1)} async-done(((bf16[1536,32]{1,0:T(8,128)(2,1)}), bf16[384,32]{1,0:T(8,128)(2,1)}) %reduce-scatter.10.cloned.1.call-update) | async-done | bytes 24592
  286.4 37.5 %psum.14 = bf16[32,384]{1,0:T(8,128)(2,1)S(1)} all-reduce(bf16[32,384]{1,0:T(8,128)(2,1)S(1)} %copy.60), channel_id=1, replica_groups=mesh['dp'=8,'tm'=4] {'dp'}, use_global_device_ids=true, to_apply=%region_43.44 | all-reduce | flops 12288 | bytes 49152 | tf_op jit(solution)/shard_map/psum | solution.py:156
  324.5 44.7 %all-reduce.2.cloned.1.call-done = bf16[384,1536]{1,0:T(8,128)(2,1)} async-done(((bf16[384,1536]{1,0:T(8,128)(2,1)}), bf16[384,1536]{1,0:T(8,128)(2,1)}) %all-reduce.2.cloned.1.call-update) | async-done | bytes 1179664 | tf_op jit(solution)/shard_map/psum | solution.py:157
  369.2 3.0 convert_element_type.368
  372.2 360.2 %all-gather.9.cloned.1.call-done = bf16[3072,3072]{1,0:T(8,128)(2,1)} async-done(((bf16[384,3072]{1,0:T(8,128)(2,1)}), bf16[3072,3072]{1,0:T(8,128)(2,1)}) %all-gather.9.cloned.1.call-update) | async-done | bytes 18874384 | tf_op jit(solution)/shard_map/all_gather | solution.py:155
  732.4 10.9 %reduce_sum.371 = bf16[384,3072]{1,0:T(8,128)(2,1)S(1)} reduce(bf16[8,384,3072]{2,1,0:T(8,128)(2,1)} %bitcast.68, bf16[]{:T(256)} %constant.33.clone.1), dimensions={0}, to_apply=%region_9.10 | reduce | flops 8257536 | bytes 21233666 | tf_op jit(solution)/shard_map/reduce_sum | solution.py:155
  743.2 2.8 convert_element_type.364
  (259 shorter events, 20.3 us)
Async XLA Ops:
  7.2 99.7 %copy-start = (bf16[1,128,1536]{2,1,0:T(8,128)(2,1)S(1)}, bf16[1,128,1536]{2,1,0:T(8,128)(2,1)}, u32[]{:S(2)}) copy-start(bf16[1,128,1536]{2,1,0:T(8,128)(2,1)} %param.19) | copy-start | bytes 1179652
  7.2 18.6 %copy-start.8 = (bf16[1,128,1536]{2,1,0:T(8,128)(2,1)S(1)}, bf16[1,128,1536]{2,1,0:T(8,128)(2,1)}, u32[]{:S(2)}) copy-start(bf16[1,128,1536]{2,1,0:T(8,128)(2,1)} %param.12) | copy-start | bytes 1179652
  7.2 83.4 %all-gather.7.cloned.1.call-start = ((), (), s32[]{:S(2)}) async-start(), calls=%async_computation.8 | async-start | bytes 11796480 | tf_op jit(solution)/shard_map/all_gather | solution.py:103
  7.9 121.7 %all-gather.5.cloned.1.call-start = ((), (), s32[]{:S(2)}) async-start(), calls=%async_computation.7 | async-start | bytes 5898240 | tf_op jit(solution)/shard_map/all_gather | solution.py:116
  10.6 11.7 %all-to-all-start.2 = ((bf16[128,4,4,96]{0,3,2,1:T(8,128)(2,1)}), bf16[128,4,4,96]{0,3,2,1:T(8,128)(2,1)S(1)}, u32[]{:S(2)}, u32[]{:S(2)}) async-start(bf16[128,4,4,96]{0,3,2,1:T(8,128)(2,1)} %bitcast.7), calls=%async_computation.2 | async-start | bytes 786432 | tf_op jit(solution)/shard_map/all_to_all | solution.py:94
  22.3 15.5 %all-to-all-start = ((bf16[128,4,4,96]{0,3,2,1:T(8,128)(2,1)}), bf16[128,4,4,96]{0,3,2,1:T(8,128)(2,1)S(1)}, u32[]{:S(2)}, u32[]{:S(2)}) async-start(bf16[128,4,4,96]{0,3,2,1:T(8,128)(2,1)} %bitcast.1), calls=%async_computation | async-start | bytes 786432 | tf_op jit(solution)/shard_map/all_to_all | solution.py:92
  37.8 15.5 %all-to-all-start.1 = ((bf16[128,4,4,96]{0,3,2,1:T(8,128)(2,1)}), bf16[128,4,4,96]{0,3,2,1:T(8,128)(2,1)S(1)}, u32[]{:S(2)}, u32[]{:S(2)}) async-start(bf16[128,4,4,96]{0,3,2,1:T(8,128)(2,1)} %bitcast.4), calls=%async_computation.1 | async-start | bytes 786432 | tf_op jit(solution)/shard_map/all_to_all | solution.py:93
  57.2 19.5 %copy-start.81 = (f32[1536]{0:T(1024)S(1)}, f32[1536]{0:T(1024)}, u32[]{:S(2)}) copy-start(f32[1536]{0:T(1024)} %param.14) | copy-start | bytes 18436
  57.2 18.4 %all-to-all-start.3 = ((bf16[512,1,4,96]{3,2,1,0:T(4,128)(2,1)}), bf16[512,1,4,96]{3,2,1,0:T(4,128)(2,1)S(1)}, u32[]{:S(2)}, u32[]{:S(2)}) async-start(bf16[512,1,4,96]{3,2,1,0:T(4,128)(2,1)} %copy.55), calls=%async_computation.3 | async-start | bytes 1048576 | tf_op jit(solution)/shard_map/all_to_all | solution.py:97
  60.8 120.4 %reduce-scatter.8.cloned.1.call-start = ((), (), s32[]{:S(2)}) async-start(), calls=%async_computation.10 | async-start | bytes 5898240 | tf_op jit(solution)/shard_map/reduce_scatter | solution.py:147
  96.2 4.7 collective-permute-start.1
  97.5 3.9 collective-permute-start
  110.7 151.0 %reduce-scatter.6.cloned.1.call-start = ((), (), s32[]{:S(2)}) async-start(), calls=%async_computation.9 | async-start | bytes 11796480 | tf_op jit(solution)/shard_map/reduce_scatter | solution.py:141
  129.6 13.4 %copy-start.13 = (f32[1536]{0:T(1024)S(1)}, f32[1536]{0:T(1024)}, u32[]{:S(2)}) copy-start(f32[1536]{0:T(1024)} %get-tuple-element.53) | copy-start | bytes 18436
  129.6 13.4 %copy-start.15 = (f32[1536]{0:T(1024)S(1)}, f32[1536]{0:T(1024)}, u32[]{:S(2)}) copy-start(f32[1536]{0:T(1024)} %get-tuple-element.54) | copy-start | bytes 18436
  129.6 13.4 %copy-start.17 = (f32[1536]{0:T(1024)S(1)}, f32[1536]{0:T(1024)}, u32[]{:S(2)}) copy-start(f32[1536]{0:T(1024)} %get-tuple-element.55) | copy-start | bytes 18436
  129.6 13.4 %copy-start.19 = (f32[1536]{0:T(1024)S(1)}, f32[1536]{0:T(1024)}, u32[]{:S(2)}) copy-start(f32[1536]{0:T(1024)} %get-tuple-element.56) | copy-start | bytes 18436
  129.6 13.4 %copy-start.21 = (f32[1536]{0:T(1024)S(1)}, f32[1536]{0:T(1024)}, u32[]{:S(2)}) copy-start(f32[1536]{0:T(1024)} %get-tuple-element.57) | copy-start | bytes 18436
  129.7 13.4 %copy-start.23 = (f32[1536]{0:T(1024)S(1)}, f32[1536]{0:T(1024)}, u32[]{:S(2)}) copy-start(f32[1536]{0:T(1024)} %get-tuple-element.58) | copy-start | bytes 18436
  129.7 13.4 %copy-start.25 = (f32[1536]{0:T(1024)S(1)}, f32[1536]{0:T(1024)}, u32[]{:S(2)}) copy-start(f32[1536]{0:T(1024)} %get-tuple-element.59) | copy-start | bytes 18436
  129.7 13.4 %copy-start.27 = (f32[1536]{0:T(1024)S(1)}, f32[1536]{0:T(1024)}, u32[]{:S(2)}) copy-start(f32[1536]{0:T(1024)} %get-tuple-element.60) | copy-start | bytes 18436
  129.7 13.4 %copy-start.29 = (f32[1536]{0:T(1024)S(1)}, f32[1536]{0:T(1024)}, u32[]{:S(2)}) copy-start(f32[1536]{0:T(1024)} %get-tuple-element.61) | copy-start | bytes 18436
  129.7 13.4 %copy-start.31 = (f32[1536]{0:T(1024)S(1)}, f32[1536]{0:T(1024)}, u32[]{:S(2)}) copy-start(f32[1536]{0:T(1024)} %get-tuple-element.62) | copy-start | bytes 18436
  129.7 13.4 %copy-start.33 = (f32[1536]{0:T(1024)S(1)}, f32[1536]{0:T(1024)}, u32[]{:S(2)}) copy-start(f32[1536]{0:T(1024)} %get-tuple-element.63) | copy-start | bytes 18436
  129.7 13.4 %copy-start.35 = (f32[1536]{0:T(1024)S(1)}, f32[1536]{0:T(1024)}, u32[]{:S(2)}) copy-start(f32[1536]{0:T(1024)} %get-tuple-element.64) | copy-start | bytes 18436
  129.7 13.4 %copy-start.37 = (f32[1536]{0:T(1024)S(1)}, f32[1536]{0:T(1024)}, u32[]{:S(2)}) copy-start(f32[1536]{0:T(1024)} %get-tuple-element.65) | copy-start | bytes 18436
  137.5 3.4 collective-permute-start.3
  139.6 3.5 collective-permute-start.2
  153.0 132.4 %reduce-scatter.10.cloned.1.call-start = ((), (), s32[]{:S(2)}) async-start(), calls=%async_computation.13 | async-start | bytes 491520
  158.4 210.9 %all-reduce.2.cloned.1.call-start = ((), (), s32[]{:S(2)}) async-start(), calls=%async_computation.11 | async-start | bytes 2359296 | tf_op jit(solution)/shard_map/psum | solution.py:157
  181.3 551.1 %all-gather.9.cloned.1.call-start = ((), (), s32[]{:S(2)}) async-start(), calls=%async_computation.12 | async-start | bytes 21233664 | tf_op jit(solution)/shard_map/all_gather | solution.py:155
  732.4 13.6 %copy-start.1 = (bf16[1,128,1536]{2,1,0:T(8,128)(2,1)S(1)}, bf16[1,128,1536]{2,1,0:T(8,128)(2,1)}, u32[]{:S(2)}) copy-start(bf16[1,128,1536]{2,1,0:T(8,128)(2,1)} %param.19) | copy-start | bytes 1179652
  (69 other events, 587.1 us)
Sparse Core Ops, SparseCore 0:
  9.6 80.9 all-gather.6
  92.1 37.4 all-gather.4
  132.7 48.4 reduce-scatter.7
  183.7 77.8 reduce-scatter.5
  264.5 20.8 reduce-scatter.9
  288.8 80.4 all-reduce.1
  370.8 361.5 all-gather.8
